TPU v7x, 256 devices: a whole 4x4x8 slice. The times are simulated.
256 devices in a mesh: dp: 32 (over x, y, core), mp: 8 (over z).
Axes of the slice: x: 4, y: 4, z: 8, core: 2. Of those that a mesh axis runs over, the one named last changes fastest.
Arguments:
- weight: bfloat16 [1024, 128, 128], P(('dp', 'mp')), may hold values from -6 to 6
- moment_one: float32 [1024, 128, 128], P(('dp', 'mp')), may hold values from -1.8 to 1.8
- moment_two: float32 [1024, 128, 128], P(('dp', 'mp')), may hold values from 0.01 to 1
- block_row: int32 [1024], P(('dp', 'mp')), may hold values from 0 to 63, as said below
- block_col: int32 [1024], P(('dp', 'mp')), may hold values from 0 to 27
- dest_slot: int32 [1024], P(('dp', 'mp')), may hold values from -1 to 127, as said below
- tokens: bfloat16 [4096, 8192], P('dp', 'mp'), may hold values from -6 to 6
- upstream: bfloat16 [4096, 28672], P('dp', 'mp'), may hold values from -6 to 6
Outputs:
- new_weight: bfloat16 [1024, 128, 128], P(('dp', 'mp'))
- new_first: float32 [1024, 128, 128], P(('dp', 'mp'))
- new_second: float32 [1024, 128, 128], P(('dp', 'mp'))
- hidden_out: bfloat16 [4096, 28672], P('dp', 'mp')
- input_grad: bfloat16 [4096, 8192], P('dp', 'mp')
Inputs may be any that keep to these rules, and one draw needn't show every extreme that they name: Within one tensor slice the pairs (block_row, block_col) are distinct. `dest_slot`: within one tensor slice the non-negative values are distinct; slots d * 4 to (d + 1) * 4 - 1 belong to dp index d, and a block held by dp index d goes to d - 1, d or d + 1; at most 2 blocks of one device go to each neighbour, and in every slice some pair of neighbours exchanges exactly 2 blocks each way.
All inputs are finite; a program needn't handle non-finite values.
Results may differ from a plain program's by a relative error of at most 0.0055.
Values may be sent and summed in bfloat16 or wider, within the bound.
A program may use at most 128 MiB of HBM per device.

v0:
```python
import math
import jax
import jax.numpy as jnp
from jax import lax
from jax.sharding import PartitionSpec as P

D = 8192
learn_rate = 0.02
beta_first = 0.9
beta_second = 0.95
epsilon = 1e-08
highest = lax.Precision.HIGHEST


def with_halo(shard, sides, width):
    for axis, dim in sides:
        size, length = (lax.axis_size(axis), shard.shape[dim])
        up = [(i, (i + 1) % size) for i in range(size - 1)]
        down = [(j, i) for i, j in up]
        last = lax.slice_in_dim(shard, length - width, length, axis=dim)
        initial = lax.slice_in_dim(shard, 0, width, axis=dim)
        before = lax.ppermute(last, axis, up)
        after = lax.ppermute(initial, axis, down)
        shard = jnp.concatenate([before, shard, after], axis=dim)
    return shard


def adam_update(gradient, weights, first_moment, second_moment):
    first_new = beta_first * first_moment + (1.0 - beta_first) * gradient
    second_new = beta_second * second_moment + (1.0 - beta_second) * gradient * gradient
    stepped = weights - learn_rate * first_new / (jnp.sqrt(second_new) + epsilon)
    return (stepped, first_new, second_new)


def moving_plan(dest_part, goal, kept_dev, half_slots):
    chosen = (dest_part >= 0) & (dest_part // kept_dev == goal)
    order_rank = jnp.cumsum(chosen.astype(jnp.int32)) - 1
    select = (
        (order_rank[None, :] == jnp.arange(half_slots, dtype=jnp.int32)[:, None]) & chosen[None, :]
    ).astype(jnp.float32)
    offsets = (
        jnp.dot(select, (dest_part % kept_dev + 1).astype(jnp.float32), precision=highest) - 1.0
    )
    return (select, offsets)


def relocate(stacked, all_dest):
    kept_dev = stacked.shape[0]
    half_slots = kept_dev // 2
    own_index = lax.axis_index("dp")
    last_index = lax.axis_size("dp") - 1
    own_dest = lax.dynamic_slice_in_dim(all_dest, own_index * kept_dev, kept_dev)
    left_dest = lax.dynamic_slice_in_dim(
        all_dest, jnp.maximum(own_index - 1, 0) * kept_dev, kept_dev
    )
    right_dest = lax.dynamic_slice_in_dim(
        all_dest, jnp.minimum(own_index + 1, last_index) * kept_dev, kept_dev
    )
    send_left, unused_left = moving_plan(own_dest, own_index - 1, kept_dev, half_slots)
    send_right, unused_right = moving_plan(own_dest, own_index + 1, kept_dev, half_slots)
    outgoing = jnp.dot(jnp.concatenate([send_left, send_right], axis=0), stacked, precision=highest)
    padded = with_halo(outgoing.astype(jnp.bfloat16), (("dp", 0),), half_slots).astype(
        outgoing.dtype
    )
    from_left = padded[:half_slots]
    from_right = padded[3 * half_slots :]
    unused_one, left_offsets = moving_plan(left_dest, own_index, kept_dev, half_slots)
    unused_two, right_offsets = moving_plan(right_dest, own_index, kept_dev, half_slots)
    left_offsets = jnp.where(own_index > 0, left_offsets, -1.0)
    right_offsets = jnp.where(own_index < last_index, right_offsets, -1.0)
    staying = (own_dest >= 0) & (own_dest // kept_dev == own_index)
    stay_offsets = jnp.where(staying, own_dest % kept_dev, -1).astype(jnp.float32)
    places = jnp.concatenate([stay_offsets, left_offsets, right_offsets])
    slot_hot = (jnp.arange(kept_dev, dtype=jnp.float32)[:, None] == places[None, :]).astype(
        jnp.float32
    )
    return jnp.dot(
        slot_hot, jnp.concatenate([stacked, from_left, from_right], axis=0), precision=highest
    )


def body(weight, moment_one, moment_two, block_row, block_col, dest_slot, tokens, upstream):
    kept_dev = weight.shape[0]
    block_side = weight.shape[1]
    flat_size = block_side * block_side
    grad_scale = 1.0 / math.sqrt(D)
    features = lax.all_gather(tokens, "mp", axis=1, tiled=True)
    all_weight, all_rows, all_cols, all_dest = (
        lax.all_gather(weight, "dp", axis=0, tiled=True),
        lax.all_gather(block_row, "dp", axis=0, tiled=True),
        lax.all_gather(block_col, "dp", axis=0, tiled=True),
        lax.all_gather(dest_slot, "dp", axis=0, tiled=True),
    )
    token_rows = features.shape[0]
    block_rows = features.shape[1] // block_side
    block_cols = upstream.shape[1] // block_side
    x_blocks = jnp.take(features.reshape(token_rows, block_rows, block_side), all_rows, axis=1)
    d_blocks = jnp.take(upstream.reshape(token_rows, block_cols, block_side), all_cols, axis=1)
    forward = jnp.einsum("tbk,bkj->btj", x_blocks, all_weight, preferred_element_type=jnp.float32)
    col_sums = jax.ops.segment_sum(forward, all_cols, num_segments=block_cols)
    hidden_out = (
        (jnp.swapaxes(col_sums, 0, 1) * grad_scale)
        .reshape(token_rows, block_cols * block_side)
        .astype(jnp.bfloat16)
    )
    backward = jnp.einsum("tbj,bkj->btk", d_blocks, all_weight, preferred_element_type=jnp.float32)
    row_sums = jax.ops.segment_sum(backward, all_rows, num_segments=block_rows)
    partial_in = (jnp.swapaxes(row_sums, 0, 1) * grad_scale).reshape(
        token_rows, block_rows * block_side
    )
    input_grad = lax.psum_scatter(partial_in, "mp", scatter_dimension=1, tiled=True).astype(
        jnp.bfloat16
    )
    old_weight = weight.reshape(kept_dev, flat_size).astype(jnp.float32)
    old_first = moment_one.reshape(kept_dev, flat_size)
    old_second = moment_two.reshape(kept_dev, flat_size)
    gradient = (
        lax.psum_scatter(
            (
                jnp.einsum("tbk,tbj->bkj", x_blocks, d_blocks, preferred_element_type=jnp.float32)
                * grad_scale
            ).astype(jnp.bfloat16),
            "dp",
            scatter_dimension=0,
            tiled=True,
        )
        .astype(jnp.float32)
        .reshape(kept_dev, flat_size)
    )
    held_weight, held_first, held_second = adam_update(gradient, old_weight, old_first, old_second)
    moved = relocate(jnp.concatenate([held_weight, held_first, held_second], axis=1), all_dest)
    stepped = moved[:, :flat_size]
    first_new = moved[:, flat_size : 2 * flat_size]
    second_new = moved[:, 2 * flat_size :]
    new_weight = stepped.astype(jnp.bfloat16).reshape(kept_dev, block_side, block_side)
    new_first = first_new.reshape(kept_dev, block_side, block_side)
    new_second = second_new.reshape(kept_dev, block_side, block_side)
    return (new_weight, new_first, new_second, hidden_out, input_grad)


def solution(mesh):
    return jax.shard_map(
        body,
        mesh=mesh,
        in_specs=(
            P(("dp", "mp"), None, None),
            P(("dp", "mp"), None, None),
            P(("dp", "mp"), None, None),
            P(("dp", "mp")),
            P(("dp", "mp")),
            P(("dp", "mp")),
            P("dp", "mp"),
            P("dp", "mp"),
        ),
        out_specs=(
            P(("dp", "mp"), None, None),
            P(("dp", "mp"), None, None),
            P(("dp", "mp"), None, None),
            P("dp", "mp"),
            P("dp", "mp"),
        ),
        check_vma=False,
    )
```

profile of v0, /device:TPU:1, one launch (start us, length us, event | category | flops | bytes accessed | tf_op | source)
XLA Modules:
  0.0 266.2 jit_solution(6325529828140879658)
XLA Ops:
  7.2 0.0 copy-start.10
  7.2 0.0 all-gather.3.cloned.1.call-start
  7.3 1.8 copy.28
  9.0 0.0 all-gather.3.cloned.1.call-update
  9.1 0.0 all-gather.5.cloned.1.call-start
  9.1 0.7 all-gather.5.cloned.1.call-update
  9.8 0.0 reduce-scatter.3.cloned.1.call-start
  9.9 1.6 copy.30
  11.4 0.6 copy.31
  12.1 0.6 dynamic-slice
  13.4 0.2 dynamic-update-slice.1
  13.6 0.2 dynamic-update-slice.2
  13.8 0.2 dynamic-update-slice
  14.1 14.4 %all-reduce.3 = (s32[128]{0:T(128)S(1)}, s32[128]{0:T(128)S(1)}, s32[128]{0:T(128)S(1)}) all-reduce(s32[128]{0:T(128)S(1)} %dynamic-update-slice.1, s32[128]{0:T(128)S(1)} %dynamic-update-slice.2, s32[128]{0:T(128)S(1)} %dynamic-update-slice), channel_id=1, replica_groups=mesh['dp'=32,'mp'=8] {'dp'}, use_global_device_ids=true, to_apply=%add.1 | all-reduce | flops 384 | bytes 3072
  28.5 3.1 %gather_fusion.1 = bf16[128,128,128]{2,1,0:T(8,128)(2,1)} fusion(bf16[128,28,128]{2,0,1:T(8,128)(2,1)S(1)} %copy.31, s32[1024]{0:T(1024)S(1)} %pad_clamp_fusion), kind=kCustom, calls=%fused_computation.1 | custom fusion | bytes 8389120 | tf_op jit(solution)/shard_map/jit(_take)/gather | solution.py:98
  31.6 19.3 %all-gather.3.cloned.1.call-done = bf16[128,8192]{0,1:T(8,128)(2,1)} async-done(((bf16[128,1024]{0,1:T(8,128)(2,1)}), bf16[128,8192]{0,1:T(8,128)(2,1)}) %all-gather.3.cloned.1.call-update) | async-done | bytes 2097168 | tf_op jit(solution)/shard_map/all_gather | solution.py:87
  50.9 3.2 %copy.29 = bf16[128,64,128]{2,0,1:T(8,128)(2,1)S(1)} copy(bf16[128,64,128]{0,2,1:T(8,128)(2,1)} %bitcast.100) | data formatting | bytes 4194304 | tf_op jit(solution)/shard_map/reshape | solution.py:97
  54.1 3.0 %gather_fusion = bf16[128,128,128]{2,1,0:T(8,128)(2,1)} fusion(bf16[128,64,128]{2,0,1:T(8,128)(2,1)S(1)} %copy.29, s32[1024]{0:T(1024)S(1)} %pad_clamp_fusion.1), kind=kCustom, calls=%fused_computation | custom fusion | bytes 8389120 | tf_op jit(solution)/shard_map/jit(_take)/gather | solution.py:97
  57.1 7.5 %multiply_convert_fusion = bf16[128,128,128]{2,1,0:T(8,128)(2,1)} fusion(bf16[128,128,128]{2,1,0:T(8,128)(2,1)} %gather_fusion, pred[128]{0:T(512)(128)(4,1)S(1)} %get-tuple-element.48, bf16[128,128,128]{2,1,0:T(8,128)(2,1)} %gather_fusion.1, pred[128]{0:T(512)(128)(4,1)S(1)} %get-tuple-element.47), kind=kOutput, calls=%fused_computation.5 | convolution fusion | flops 545259520 | bytes 12583168 | tf_op jit(solution)/shard_map/tbk,tbj->bkj/dot_general | solution.py:120
  64.6 0.0 reduce-scatter.3.cloned.1.call-update
  64.6 0.2 reduce-scatter.5.cloned.1.call-start
  64.9 0.1 fusion.53
  65.0 0.2 reduce-window.35
  65.1 0.2 reduce-window.34
  65.3 0.1 convert_bitcast_fusion.5
  65.4 0.2 reduce-window.33
  65.6 0.2 reduce-window.32
  65.8 0.2 fusion.24
  66.0 0.2 fusion.22
  66.2 0.1 pad_maximum_fusion.2
  66.4 41.3 %all-gather.5.cloned.1.call-done = bf16[128,128,128]{2,1,0:T(8,128)(2,1)} async-done(((bf16[4,128,128]{2,1,0:T(8,128)(2,1)}), bf16[128,128,128]{2,1,0:T(8,128)(2,1)}) %all-gather.5.cloned.1.call-update) | async-done | bytes 4194320 | tf_op jit(solution)/shard_map/all_gather | solution.py:89
  107.7 9.8 %fusion = f32[128,128,128]{2,1,0:T(8,128)} fusion(bf16[128,128,128]{2,1,0:T(8,128)(2,1)} %all-gather.5.cloned.1.call-done, bf16[128,128,128]{2,1,0:T(8,128)(2,1)} %gather_fusion.1, pred[128]{0:T(512)(128)(4,1)S(1)} %get-tuple-element.47), kind=kOutput, calls=%fused_computation.6 | convolution fusion | flops 538968064 | bytes 16777344 | tf_op jit(solution)/shard_map/tbj,bkj->btk/dot_general | solution.py:106
  117.4 2.5 broadcast_in_dim.60
  119.9 27.1 %scatter_fusion.1 = f32[64,128,128]{2,1,0:T(8,128)} fusion(f32[64,128,128]{2,1,0:T(8,128)} %broadcast_in_dim.60, s32[128]{0:T(128)S(1)} %get-tuple-element.20, f32[128,128,128]{2,1,0:T(8,128)} %fusion), kind=kCustom, calls=%fused_computation.3 | custom fusion | flops 2097152 | bytes 25166336 | tf_op jit(solution)/shard_map/scatter-add | solution.py:107
  147.0 5.0 %multiply_bitcast_fusion = f32[128,64,128]{2,0,1:T(8,128)} fusion(f32[64,128,128]{2,1,0:T(8,128)} %scatter_fusion.1), kind=kLoop, calls=%fused_computation.13 | loop fusion | flops 1048576 | bytes 8388608 | tf_op jit(solution)/shard_map/mul | solution.py:108
  152.0 5.6 %copy.34 = f32[128,64,128]{0,2,1:T(8,128)} copy(f32[128,64,128]{2,0,1:T(8,128)} %multiply_bitcast_fusion) | data formatting | bytes 8388608 | tf_op jit(solution)/shard_map/mul | solution.py:108
  157.6 8.0 %fusion.4 = f32[128,128,128]{2,1,0:T(8,128)} fusion(bf16[128,128,128]{2,1,0:T(8,128)(2,1)} %all-gather.5.cloned.1.call-done, bf16[128,128,128]{2,1,0:T(8,128)(2,1)} %gather_fusion, pred[128]{0:T(512)(128)(4,1)S(1)} %get-tuple-element.48), kind=kOutput, calls=%fused_computation.10 | convolution fusion | flops 538968064 | bytes 16777344 | tf_op jit(solution)/shard_map/tbk,bkj->btj/dot_general | solution.py:99
  165.6 0.2 broadcast_in_dim.58
  165.8 17.2 %scatter_fusion = f32[28,128,128]{2,1,0:T(8,128)S(1)} fusion(f32[28,128,128]{2,1,0:T(8,128)S(1)} %broadcast_in_dim.58, s32[128]{0:T(128)S(1)} %get-tuple-element.21, f32[128,128,128]{2,1,0:T(8,128)} %fusion.4), kind=kCustom, calls=%fused_computation.2 | custom fusion | flops 2097152 | bytes 25166336 | tf_op jit(solution)/shard_map/scatter-add | solution.py:100
  183.0 0.0 reduce-scatter.5.cloned.1.call-update
  183.0 15.9 %reduce-scatter.3.cloned.1.call-done = bf16[4,128,128]{2,1,0:T(8,128)(2,1)} async-done(((bf16[128,128,128]{2,1,0:T(8,128)(2,1)}), bf16[4,128,128]{2,1,0:T(8,128)(2,1)}) %reduce-scatter.3.cloned.1.call-update) | async-done | bytes 131088 | tf_op jit(solution)/shard_map/reduce_scatter | solution.py:118
  198.9 0.9 convert_bitcast_fusion
  199.9 0.8 bitcast_subtract_fusion
  200.7 0.0 copy-start.1
  200.7 0.0 copy-start.3
  200.7 0.9 convolution_convert_fusion
  201.6 1.0 fusion.74
  202.7 4.3 %collective-permute-start.1 = (bf16[2,49152]{1,0:T(2,128)(2,1)}, bf16[2,49152]{1,0:T(2,128)(2,1)}, u32[]{:S(2)}, u32[]{:S(2)}) collective-permute-start(bf16[2,49152]{1,0:T(2,128)(2,1)} %get-tuple-element.42), channel_id=1, source_target_pairs={{8,0},{16,8},{24,16},{32,24},{40,32},{48,40},{56,48},{64,56},{72,6... | collective-permute-start | bytes 589832 | tf_op jit(solution)/shard_map/ppermute | solution.py:23
  206.9 2.9 %collective-permute-start = (bf16[2,49152]{1,0:T(2,128)(2,1)}, bf16[2,49152]{1,0:T(2,128)(2,1)}, u32[]{:S(2)}, u32[]{:S(2)}) collective-permute-start(bf16[2,49152]{1,0:T(2,128)(2,1)} %get-tuple-element.41), channel_id=1, source_target_pairs={{0,8},{8,16},{16,24},{24,32},{32,40},{40,48},{48,56},{56,64},{64,7... | collective-permute-start | bytes 589832 | tf_op jit(solution)/shard_map/ppermute | solution.py:22
  209.9 0.3 fusion.25
  210.1 0.0 copy-start.2
  210.1 0.0 copy-start.4
  210.2 0.6 copy.33
  210.8 1.3 copy.35
  212.1 0.0 collective-permute-done.1
  212.1 0.5 collective-permute-done
  212.6 2.4 maximum_convert_fusion
  215.0 1.3 fusion.11
  216.3 0.7 copy.59
  217.0 0.7 copy.58
  217.7 0.7 copy.57
  218.4 39.3 %reduce-scatter.5.cloned.1.call-done = f32[128,1024]{0,1:T(8,128)} async-done(((f32[128,8192]{0,1:T(8,128)}), f32[128,1024]{0,1:T(8,128)}) %reduce-scatter.5.cloned.1.call-update) | async-done | bytes 524304 | tf_op jit(solution)/shard_map/reduce_scatter | solution.py:111
  257.8 1.1 convert_element_type.58
  258.9 0.9 copy.36
  (35 shorter events, 0.3 us)
Async XLA Ops:
  7.2 4.9 %copy-start.10 = (u32[256]{0:T(256)S(1)}, u32[256]{0:T(256)}, u32[]{:S(2)}) copy-start(u32[256]{0:T(256)} %constant.143) | copy-start | bytes 3076
  7.2 6.2 %copy-start.7 = (s32[4]{0:T(128)S(1)}, s32[4]{0:T(128)}, u32[]{:S(2)}) copy-start(s32[4]{0:T(128)} %param.11) | copy-start | bytes 52
  7.2 6.4 %copy-start.8 = (s32[4]{0:T(128)S(1)}, s32[4]{0:T(128)}, u32[]{:S(2)}) copy-start(s32[4]{0:T(128)} %param.12) | copy-start | bytes 52
  7.2 6.6 %copy-start.9 = (s32[4]{0:T(128)S(1)}, s32[4]{0:T(128)}, u32[]{:S(2)}) copy-start(s32[4]{0:T(128)} %param.13) | copy-start | bytes 52
  7.2 43.7 %all-gather.3.cloned.1.call-start = ((), (), s32[]{:S(2)}) async-start(), calls=%async_computation.2 | async-start | bytes 2359296 | tf_op jit(solution)/shard_map/all_gather | solution.py:87
  9.1 98.6 %all-gather.5.cloned.1.call-start = ((), (), s32[]{:S(2)}) async-start(), calls=%async_computation.4 | async-start | bytes 4325376 | tf_op jit(solution)/shard_map/all_gather | solution.py:89
  9.8 189.1 %reduce-scatter.3.cloned.1.call-start = ((), (), s32[]{:S(2)}) async-start(), calls=%async_computation.3 | async-start | bytes 4325376 | tf_op jit(solution)/shard_map/reduce_scatter | solution.py:118
  64.6 1.7 copy-start
  64.6 1.7 copy-start.5
  64.6 1.8 copy-start.6
  64.6 193.2 %reduce-scatter.5.cloned.1.call-start = ((), (), s32[]{:S(2)}) async-start(), calls=%async_computation.5 | async-start | bytes 4718592 | tf_op jit(solution)/shard_map/reduce_scatter | solution.py:111
  200.7 6.3 %copy-start.1 = (f32[4,16384]{1,0:T(4,128)}, f32[4,16384]{1,0:T(4,128)S(1)}, u32[]{:S(2)}) copy-start(f32[4,16384]{1,0:T(4,128)S(1)} %get-tuple-element.35) | copy-start | bytes 786436
  200.7 6.3 %copy-start.3 = (f32[4,16384]{1,0:T(4,128)}, f32[4,16384]{1,0:T(4,128)S(1)}, u32[]{:S(2)}) copy-start(f32[4,16384]{1,0:T(4,128)S(1)} %get-tuple-element.36) | copy-start | bytes 786436
  202.7 9.4 %collective-permute-start.1 = (bf16[2,49152]{1,0:T(2,128)(2,1)}, bf16[2,49152]{1,0:T(2,128)(2,1)}, u32[]{:S(2)}, u32[]{:S(2)}) collective-permute-start(bf16[2,49152]{1,0:T(2,128)(2,1)} %get-tuple-element.42), channel_id=1, source_target_pairs={{8,0},{16,8},{24,16},{32,24},{40,32},{48,40},{56,48},{64,56},{72,6... | collective-permute-start | bytes 589832 | tf_op jit(solution)/shard_map/ppermute | solution.py:23
  206.9 5.6 %collective-permute-start = (bf16[2,49152]{1,0:T(2,128)(2,1)}, bf16[2,49152]{1,0:T(2,128)(2,1)}, u32[]{:S(2)}, u32[]{:S(2)}) collective-permute-start(bf16[2,49152]{1,0:T(2,128)(2,1)} %get-tuple-element.41), channel_id=1, source_target_pairs={{0,8},{8,16},{16,24},{24,32},{32,40},{40,48},{48,56},{56,64},{64,7... | collective-permute-start | bytes 589832 | tf_op jit(solution)/shard_map/ppermute | solution.py:22
  210.1 4.8 %copy-start.2 = (f32[4,16384]{1,0:T(4,128)S(1)}, f32[4,16384]{1,0:T(4,128)}, u32[]{:S(2)}) copy-start(f32[4,16384]{1,0:T(4,128)} %copy-done.1) | copy-start | bytes 786436
  210.1 4.8 %copy-start.4 = (f32[4,16384]{1,0:T(4,128)S(1)}, f32[4,16384]{1,0:T(4,128)}, u32[]{:S(2)}) copy-start(f32[4,16384]{1,0:T(4,128)} %copy-done.3) | copy-start | bytes 786436
Sparse Core Ops, SparseCore 0:
  10.4 40.4 all-gather.2
  53.4 54.1 all-gather.4
  111.6 87.2 reduce-scatter.2
  201.3 56.3 reduce-scatter.4
where the time goes:
time: 267 us; the launch traced here: 266 us
  waiting for transfers between devices  117 us (44%)
  other arithmetic  55.8 us (21%)
  local copies, waits for them, and re-layouts  28.9 us (11%)
  matrix products  27.8 us (10%)
  between operations  14.8 us (6%)
  blocking collectives  14.4 us (5%)
  starting transfers between devices  7.52 us (3%)
    all_gather x1, waiting for transfers between devices, body(): lax.all_gather(weight, 'dp', axis=0, tiled=True)  41.3 us
    reduce_scatter x1, waiting for transfers between devices, body(): lax.psum_scatter(partial_in, 'mp', scatter_dimension=1, tiled=True)  39.3 us
    scatter-add x1, other arithmetic, body(): row_sums = jax.ops.segment_sum(backward, all_rows, num_segments=block_rows)  27.1 us
    all_gather x1, waiting for transfers between devices, body(): features = lax.all_gather(tokens, 'mp', axis=1, tiled=True)  19.3 us
    scatter-add x1, other arithmetic, body(): col_sums = jax.ops.segment_sum(forward, all_cols, num_segments=block_cols)  17.2 us
    reduce_scatter x1, waiting for transfers between devices, body(): lax.psum_scatter((jnp.einsum('tbk,tbj->bkj', x_blocks, d_blocks, preferre...  15.9 us
    unnamed x1, blocking collectives  14.4 us
    dot_general x1, matrix products, body(): jnp.einsum('tbj,bkj->btk', d_blocks, all_weight, preferred_element_type=j...  9.78 us
  transfers between devices with their start and end apart: 6, of which 5 were waited for; matrix products, arithmetic and copies ran while one was open for 41% of the time, Pallas kernels for 0%

commit v1 on v0

--- a/solution.py
+++ b/solution.py
@@ -86,7 +86,9 @@
     grad_scale = 1.0 / math.sqrt(D)
     features = lax.all_gather(tokens, "mp", axis=1, tiled=True)
     all_weight, all_rows, all_cols, all_dest = (
-        lax.all_gather(weight, "dp", axis=0, tiled=True),
+        jnp.concatenate(
+            lax.all_to_all(jnp.stack([weight] * lax.axis_size("dp")), "dp", 0, 0), axis=0
+        ),
         lax.all_gather(block_row, "dp", axis=0, tiled=True),
         lax.all_gather(block_col, "dp", axis=0, tiled=True),
         lax.all_gather(dest_slot, "dp", axis=0, tiled=True),

time: 267 us -> 276 us (1.034)
  starting transfers between devices: 7.52 us -> 20.3 us
  waiting for transfers between devices: 117 us -> 110 us
  local copies, waits for them, and re-layouts: 28.9 us -> 32.6 us
    all_to_all x0 -> x1, waiting for transfers between devices: none -> 57.3 us  [body(): lax.all_to_all(jnp.stack([weight] * lax.axis_size('dp')), 'dp', 0, 0)]
    all_gather x1 -> x0, waiting for transfers between devices: 41.3 us -> none  [body(): lax.all_gather(weight, 'dp', axis=0, tiled=True)]
    reduce_scatter x1, waiting for transfers between devices: 15.9 us -> 0.02 us  [body(): lax.psum_scatter((jnp.einsum('tbk,tbj->bkj', x_blocks, d_blocks, preferre...]
    all_to_all x0 -> x1, starting transfers between devices: none -> 11.9 us  [body(): lax.all_to_all(jnp.stack([weight] * lax.axis_size('dp')), 'dp', 0, 0)]
    reduce_scatter x1, waiting for transfers between devices: 39.3 us -> 31.8 us  [body(): lax.psum_scatter(partial_in, 'mp', scatter_dimension=1, tiled=True)]
    another operation x0 -> x1, local copies, waits for them, and re-layouts: none -> 2.98 us  [body(): jnp.stack([weight] * lax.axis_size('dp'))]
  transfers between devices with their start and end apart: 6 -> 6, of which waited for: 5 -> 4; matrix products, arithmetic and copies ran while one was open for 41% -> 35% of each run, Pallas kernels for 0% -> 0%
where the time goes in v1:
time: 276 us; the launch traced here: 275 us
  waiting for transfers between devices  110 us (40%)
  other arithmetic  55 us (20%)
  local copies, waits for them, and re-layouts  32.6 us (12%)
  matrix products  28 us (10%)
  starting transfers between devices  20.3 us (7%)
  between operations  14.8 us (5%)
  blocking collectives  14.4 us (5%)
    all_to_all x1, waiting for transfers between devices, body(): lax.all_to_all(jnp.stack([weight] * lax.axis_size('dp')), 'dp', 0, 0)  57.3 us
    reduce_scatter x1, waiting for transfers between devices, body(): lax.psum_scatter(partial_in, 'mp', scatter_dimension=1, tiled=True)  31.8 us
    scatter-add x1, other arithmetic, body(): row_sums = jax.ops.segment_sum(backward, all_rows, num_segments=block_rows)  26.5 us
    all_gather x1, waiting for transfers between devices, body(): features = lax.all_gather(tokens, 'mp', axis=1, tiled=True)  20.1 us
    scatter-add x1, other arithmetic, body(): col_sums = jax.ops.segment_sum(forward, all_cols, num_segments=block_cols)  17.1 us
    unnamed x1, blocking collectives  14.4 us
    all_to_all x1, starting transfers between devices, body(): lax.all_to_all(jnp.stack([weight] * lax.axis_size('dp')), 'dp', 0, 0)  11.9 us
    dot_general x1, matrix products, body(): jnp.einsum('tbj,bkj->btk', d_blocks, all_weight, preferred_element_type=j...  9.91 us
  transfers between devices with their start and end apart: 6, of which 4 were waited for; matrix products, arithmetic and copies ran while one was open for 35% of the time, Pallas kernels for 0%

profile of v1, /device:TPU:1, one launch (start us, length us, event | category | flops | bytes accessed | tf_op | source)
XLA Modules:
  0.0 274.8 jit_solution(7096065754359575980)
XLA Ops:
  7.2 0.0 copy-start.10
  7.2 0.0 all-gather.2.cloned.1.call-start
  7.3 1.8 copy.19
  9.0 0.0 all-gather.2.cloned.1.call-update
  9.1 0.0 reduce-scatter.3.cloned.1.call-start
  9.1 1.6 copy.21
  10.7 0.6 copy.22
  11.4 0.6 dynamic-slice
  12.6 0.2 dynamic-update-slice.1
  12.9 0.2 dynamic-update-slice.2
  13.1 0.2 dynamic-update-slice
  13.3 14.4 %all-reduce.3 = (s32[128]{0:T(128)S(1)}, s32[128]{0:T(128)S(1)}, s32[128]{0:T(128)S(1)}) all-reduce(s32[128]{0:T(128)S(1)} %dynamic-update-slice.1, s32[128]{0:T(128)S(1)} %dynamic-update-slice.2, s32[128]{0:T(128)S(1)} %dynamic-update-slice), channel_id=1, replica_groups=mesh['dp'=32,'mp'=8] {'dp'}, use_global_device_ids=true, to_apply=%add.1 | all-reduce | flops 384 | bytes 3072
  27.8 3.0 %gather_fusion.1 = bf16[128,128,128]{2,1,0:T(8,128)(2,1)} fusion(bf16[128,28,128]{2,0,1:T(8,128)(2,1)S(1)} %copy.22, s32[1024]{0:T(1024)S(1)} %pad_clamp_fusion), kind=kCustom, calls=%fused_computation.1 | custom fusion | bytes 8389120 | tf_op jit(solution)/shard_map/jit(_take)/gather | solution.py:100
  30.8 20.1 %all-gather.2.cloned.1.call-done = bf16[128,8192]{0,1:T(8,128)(2,1)} async-done(((bf16[128,1024]{0,1:T(8,128)(2,1)}), bf16[128,8192]{0,1:T(8,128)(2,1)}) %all-gather.2.cloned.1.call-update) | async-done | bytes 2097168 | tf_op jit(solution)/shard_map/all_gather | solution.py:87
  50.9 3.2 %copy.20 = bf16[128,64,128]{2,0,1:T(8,128)(2,1)S(1)} copy(bf16[128,64,128]{0,2,1:T(8,128)(2,1)} %bitcast.101) | data formatting | bytes 4194304 | tf_op jit(solution)/shard_map/reshape | solution.py:99
  54.1 3.0 %gather_fusion = bf16[128,128,128]{2,1,0:T(8,128)(2,1)} fusion(bf16[128,64,128]{2,0,1:T(8,128)(2,1)S(1)} %copy.20, s32[1024]{0:T(1024)S(1)} %pad_clamp_fusion.1), kind=kCustom, calls=%fused_computation | custom fusion | bytes 8389120 | tf_op jit(solution)/shard_map/jit(_take)/gather | solution.py:99
  57.1 7.5 %multiply_convert_fusion = bf16[128,128,128]{2,1,0:T(8,128)(2,1)} fusion(bf16[128,128,128]{2,1,0:T(8,128)(2,1)} %gather_fusion, pred[128]{0:T(512)(128)(4,1)S(1)} %get-tuple-element.43, bf16[128,128,128]{2,1,0:T(8,128)(2,1)} %gather_fusion.1, pred[128]{0:T(512)(128)(4,1)S(1)} %get-tuple-element.42), kind=kOutput, calls=%fused_computation.5 | convolution fusion | flops 545259520 | bytes 12583168 | tf_op jit(solution)/shard_map/tbk,tbj->bkj/dot_general | solution.py:122
  64.6 0.0 reduce-scatter.3.cloned.1.call-update
  64.6 0.9 copy-done
  65.5 3.0 %stack.2 = bf16[32,4,128,128]{3,2,1,0:T(8,128)(2,1)} broadcast(bf16[4,128,128]{2,1,0:T(8,128)(2,1)S(1)} %copy-done), dimensions={1,2,3} | broadcast | bytes 4325376 | tf_op jit(solution)/shard_map/stack | solution.py:90
  68.5 11.9 %all-to-all-start = ((bf16[32,4,128,128]{3,2,1,0:T(8,128)(2,1)}), bf16[32,4,128,128]{3,2,1,0:T(8,128)(2,1)}, u32[]{:S(2)}, u32[]{:S(2)}) async-start(bf16[32,4,128,128]{3,2,1,0:T(8,128)(2,1)} %stack.2), calls=%async_computation.1 | async-start | bytes 8388608 | tf_op jit(solution)/shard_map/all_to_all | solution.py:90
  80.4 0.2 reduce-scatter.5.cloned.1.call-start
  80.7 0.1 fusion.53
  80.8 0.2 reduce-window.35
  80.9 0.2 reduce-window.34
  81.1 0.1 convert_bitcast_fusion.5
  81.2 0.2 reduce-window.33
  81.4 0.2 reduce-window.32
  81.6 0.2 fusion.24
  81.8 0.2 fusion.22
  82.0 0.1 pad_maximum_fusion.2
  82.2 57.3 %all-to-all-done = bf16[32,4,128,128]{3,2,1,0:T(8,128)(2,1)} async-done(((bf16[32,4,128,128]{3,2,1,0:T(8,128)(2,1)}), bf16[32,4,128,128]{3,2,1,0:T(8,128)(2,1)}, u32[]{:S(2)}, u32[]{:S(2)}) %all-to-all-start) | async-done | bytes 4194336 | tf_op jit(solution)/shard_map/all_to_all | solution.py:90
  139.5 9.9 %fusion = f32[128,128,128]{2,1,0:T(8,128)} fusion(bf16[128,128,128]{2,1,0:T(8,128)(2,1)} %bitcast.17, bf16[128,128,128]{2,1,0:T(8,128)(2,1)} %gather_fusion.1, pred[128]{0:T(512)(128)(4,1)S(1)} %get-tuple-element.42), kind=kOutput, calls=%fused_computation.6 | convolution fusion | flops 538968064 | bytes 16777344 | tf_op jit(solution)/shard_map/tbj,bkj->btk/dot_general | solution.py:108
  149.4 2.4 broadcast_in_dim.60
  151.8 26.5 %scatter_fusion.1 = f32[64,128,128]{2,1,0:T(8,128)} fusion(f32[64,128,128]{2,1,0:T(8,128)} %broadcast_in_dim.60, s32[128]{0:T(128)S(1)} %get-tuple-element.15, f32[128,128,128]{2,1,0:T(8,128)} %fusion), kind=kCustom, calls=%fused_computation.3 | custom fusion | flops 2097152 | bytes 25166336 | tf_op jit(solution)/shard_map/scatter-add | solution.py:109
  178.4 4.9 %multiply_bitcast_fusion = f32[128,64,128]{2,0,1:T(8,128)} fusion(f32[64,128,128]{2,1,0:T(8,128)} %scatter_fusion.1), kind=kLoop, calls=%fused_computation.13 | loop fusion | flops 1048576 | bytes 8388608 | tf_op jit(solution)/shard_map/mul | solution.py:110
  183.2 5.6 %copy.25 = f32[128,64,128]{0,2,1:T(8,128)} copy(f32[128,64,128]{2,0,1:T(8,128)} %multiply_bitcast_fusion) | data formatting | bytes 8388608 | tf_op jit(solution)/shard_map/mul | solution.py:110
  188.8 8.0 %fusion.4 = f32[128,128,128]{2,1,0:T(8,128)} fusion(bf16[128,128,128]{2,1,0:T(8,128)(2,1)} %bitcast.17, bf16[128,128,128]{2,1,0:T(8,128)(2,1)} %gather_fusion, pred[128]{0:T(512)(128)(4,1)S(1)} %get-tuple-element.43), kind=kOutput, calls=%fused_computation.10 | convolution fusion | flops 538968064 | bytes 16777344 | tf_op jit(solution)/shard_map/tbk,bkj->btj/dot_general | solution.py:101
  196.8 0.2 broadcast_in_dim.58
  197.0 17.1 %scatter_fusion = f32[28,128,128]{2,1,0:T(8,128)S(1)} fusion(f32[28,128,128]{2,1,0:T(8,128)S(1)} %broadcast_in_dim.58, s32[128]{0:T(128)S(1)} %get-tuple-element.16, f32[128,128,128]{2,1,0:T(8,128)} %fusion.4), kind=kCustom, calls=%fused_computation.2 | custom fusion | flops 2097152 | bytes 25166336 | tf_op jit(solution)/shard_map/scatter-add | solution.py:102
  214.1 0.0 reduce-scatter.5.cloned.1.call-update
  214.1 0.0 reduce-scatter.3.cloned.1.call-done
  214.2 0.9 convert_bitcast_fusion
  215.1 0.8 bitcast_subtract_fusion
  215.9 0.0 copy-start.1
  215.9 0.0 copy-start.3
  215.9 0.9 convolution_convert_fusion
  216.8 1.0 fusion.74
  217.9 3.9 %collective-permute-start.1 = (bf16[2,49152]{1,0:T(2,128)(2,1)}, bf16[2,49152]{1,0:T(2,128)(2,1)}, u32[]{:S(2)}, u32[]{:S(2)}) collective-permute-start(bf16[2,49152]{1,0:T(2,128)(2,1)} %get-tuple-element.37), channel_id=1, source_target_pairs={{8,0},{16,8},{24,16},{32,24},{40,32},{48,40},{56,48},{64,56},{72,6... | collective-permute-start | bytes 589832 | tf_op jit(solution)/shard_map/ppermute | solution.py:23
  221.8 4.2 %collective-permute-start = (bf16[2,49152]{1,0:T(2,128)(2,1)}, bf16[2,49152]{1,0:T(2,128)(2,1)}, u32[]{:S(2)}, u32[]{:S(2)}) collective-permute-start(bf16[2,49152]{1,0:T(2,128)(2,1)} %get-tuple-element.36), channel_id=1, source_target_pairs={{0,8},{8,16},{16,24},{24,32},{32,40},{40,48},{48,56},{56,64},{64,7... | collective-permute-start | bytes 589832 | tf_op jit(solution)/shard_map/ppermute | solution.py:22
  226.0 0.3 fusion.25
  226.3 0.0 copy-start.2
  226.3 0.0 copy-start.4
  226.3 0.6 copy.24
  227.0 1.3 copy.26
  228.2 0.5 collective-permute-done
  228.7 2.4 maximum_convert_fusion
  231.1 1.3 fusion.11
  232.4 0.7 copy.50
  233.1 0.7 copy.49
  233.9 0.7 copy.48
  234.6 31.8 %reduce-scatter.5.cloned.1.call-done = f32[128,1024]{0,1:T(8,128)} async-done(((f32[128,8192]{0,1:T(8,128)}), f32[128,1024]{0,1:T(8,128)}) %reduce-scatter.5.cloned.1.call-update) | async-done | bytes 524304 | tf_op jit(solution)/shard_map/reduce_scatter | solution.py:113
  266.4 1.1 convert_element_type.58
  267.4 0.9 copy.27
  (35 shorter events, 0.3 us)
Async XLA Ops:
  7.2 4.2 %copy-start.10 = (u32[256]{0:T(256)S(1)}, u32[256]{0:T(256)}, u32[]{:S(2)}) copy-start(u32[256]{0:T(256)} %constant.143) | copy-start | bytes 3076
  7.2 5.4 %copy-start.7 = (s32[4]{0:T(128)S(1)}, s32[4]{0:T(128)}, u32[]{:S(2)}) copy-start(s32[4]{0:T(128)} %param.11) | copy-start | bytes 52
  7.2 5.7 %copy-start.8 = (s32[4]{0:T(128)S(1)}, s32[4]{0:T(128)}, u32[]{:S(2)}) copy-start(s32[4]{0:T(128)} %param.12) | copy-start | bytes 52
  7.2 5.9 %copy-start.9 = (s32[4]{0:T(128)S(1)}, s32[4]{0:T(128)}, u32[]{:S(2)}) copy-start(s32[4]{0:T(128)} %param.13) | copy-start | bytes 52
  7.2 43.7 %all-gather.2.cloned.1.call-start = ((), (), s32[]{:S(2)}) async-start(), calls=%async_computation.3 | async-start | bytes 2359296 | tf_op jit(solution)/shard_map/all_gather | solution.py:87
  9.1 205.1 %reduce-scatter.3.cloned.1.call-start = ((), (), s32[]{:S(2)}) async-start(), calls=%async_computation.4 | async-start | bytes 4325376 | tf_op jit(solution)/shard_map/reduce_scatter | solution.py:120
  64.6 0.9 copy-start
  68.5 13.6 %copy-start.5 = (f32[4,128,128]{2,1,0:T(8,128)S(1)}, f32[4,128,128]{2,1,0:T(8,128)}, u32[]{:S(2)}) copy-start(f32[4,128,128]{2,1,0:T(8,128)} %param.10) | copy-start | bytes 786436
  68.5 13.6 %copy-start.6 = (f32[4,128,128]{2,1,0:T(8,128)S(1)}, f32[4,128,128]{2,1,0:T(8,128)}, u32[]{:S(2)}) copy-start(f32[4,128,128]{2,1,0:T(8,128)} %param.9) | copy-start | bytes 786436
  68.5 71.0 %all-to-all-start = ((bf16[32,4,128,128]{3,2,1,0:T(8,128)(2,1)}), bf16[32,4,128,128]{3,2,1,0:T(8,128)(2,1)}, u32[]{:S(2)}, u32[]{:S(2)}) async-start(bf16[32,4,128,128]{3,2,1,0:T(8,128)(2,1)} %stack.2), calls=%async_computation.1 | async-start | bytes 8388608 | tf_op jit(solution)/shard_map/all_to_all | solution.py:90
  80.4 185.9 %reduce-scatter.5.cloned.1.call-start = ((), (), s32[]{:S(2)}) async-start(), calls=%async_computation.5 | async-start | bytes 4718592 | tf_op jit(solution)/shard_map/reduce_scatter | solution.py:113
  215.9 5.9 %copy-start.1 = (f32[4,16384]{1,0:T(4,128)}, f32[4,16384]{1,0:T(4,128)S(1)}, u32[]{:S(2)}) copy-start(f32[4,16384]{1,0:T(4,128)S(1)} %get-tuple-element.30) | copy-start | bytes 786436
  215.9 5.9 %copy-start.3 = (f32[4,16384]{1,0:T(4,128)}, f32[4,16384]{1,0:T(4,128)S(1)}, u32[]{:S(2)}) copy-start(f32[4,16384]{1,0:T(4,128)S(1)} %get-tuple-element.31) | copy-start | bytes 786436
  217.9 10.4 %collective-permute-start.1 = (bf16[2,49152]{1,0:T(2,128)(2,1)}, bf16[2,49152]{1,0:T(2,128)(2,1)}, u32[]{:S(2)}, u32[]{:S(2)}) collective-permute-start(bf16[2,49152]{1,0:T(2,128)(2,1)} %get-tuple-element.37), channel_id=1, source_target_pairs={{8,0},{16,8},{24,16},{32,24},{40,32},{48,40},{56,48},{64,56},{72,6... | collective-permute-start | bytes 589832 | tf_op jit(solution)/shard_map/ppermute | solution.py:23
  221.8 6.9 %collective-permute-start = (bf16[2,49152]{1,0:T(2,128)(2,1)}, bf16[2,49152]{1,0:T(2,128)(2,1)}, u32[]{:S(2)}, u32[]{:S(2)}) collective-permute-start(bf16[2,49152]{1,0:T(2,128)(2,1)} %get-tuple-element.36), channel_id=1, source_target_pairs={{0,8},{8,16},{16,24},{24,32},{32,40},{40,48},{48,56},{56,64},{64,7... | collective-permute-start | bytes 589832 | tf_op jit(solution)/shard_map/ppermute | solution.py:22
  226.3 4.8 %copy-start.2 = (f32[4,16384]{1,0:T(4,128)S(1)}, f32[4,16384]{1,0:T(4,128)}, u32[]{:S(2)}) copy-start(f32[4,16384]{1,0:T(4,128)} %copy-done.1) | copy-start | bytes 786436
  226.3 4.8 %copy-start.4 = (f32[4,16384]{1,0:T(4,128)S(1)}, f32[4,16384]{1,0:T(4,128)}, u32[]{:S(2)}) copy-start(f32[4,16384]{1,0:T(4,128)} %copy-done.3) | copy-start | bytes 786436
Sparse Core Ops, SparseCore 0:
  10.4 40.4 all-gather.1
  64.8 96.2 reduce-scatter.2
  214.2 52.0 reduce-scatter.4
